TPU v7x, 256 devices: a whole 4x4x8 slice. The times are simulated.
256 devices in a mesh: row: 8 (over x, core), col: 4 (over z_lo), layer: 8 (over y, z_hi).
Axes of the slice: x: 4, y: 4, z: 8 (z_hi: 2, z_lo: 4; z = z_hi * 4 + z_lo), core: 2. Of those that a mesh axis runs over, the one named last changes fastest.
Arguments:
- a_tiles: bfloat16 [8192, 16384], P('row', ('layer', 'col')), may hold values from -6 to 6
- a_occupancy: int32 [64, 128], P('row', ('layer', 'col')), may hold values 0 or 1
- b_tiles: bfloat16 [16384, 8192], P(('layer', 'row'), 'col'), may hold values from -0.046875 to 0.046875
- b_occupancy: int32 [128, 64], P(('layer', 'row'), 'col'), may hold values 0 or 1
Outputs:
- product: float32 [8192, 8192], P(('row', 'layer'), 'col')
Inputs may be any that keep to these rules, and one draw needn't show every extreme that they name: `a_occupancy`: each entry is 0 (block absent) or 1 (block present). `b_occupancy`: each entry is 0 (block absent) or 1 (block present).
All inputs are finite; a program needn't handle non-finite values.
Results may differ from a plain program's by a relative error of at most 0.0003.
Values may be sent and summed in bfloat16 or wider, within the bound.
A program may use at most 64 MiB of HBM per device.

v0:
```python
import jax
import jax.numpy as jnp
from jax import lax
from jax.sharding import PartitionSpec as P

BLOCK = 128


def keep_blocks(values, occupancy):
    height, breadth = values.shape
    tiled = values.reshape(height // BLOCK, BLOCK, breadth // BLOCK, BLOCK)
    flags = occupancy.astype(values.dtype)
    return (tiled * flags[:, None, :, None]).reshape(height, breadth)


def per_device(a_tiles, a_occupancy, b_tiles, b_occupancy):
    a_kept = keep_blocks(a_tiles, a_occupancy)
    b_kept = keep_blocks(b_tiles, b_occupancy)
    b_slab = lax.all_gather(b_kept, "row", axis=0, tiled=True)
    partial_value = jnp.dot(
        lax.all_gather(a_kept, "col", axis=1, tiled=True),
        b_slab,
        preferred_element_type=jnp.float32,
    )
    return lax.psum_scatter(partial_value, "layer", scatter_dimension=0, tiled=True)


def solution(mesh):
    in_specs = (
        P("row", ("layer", "col")),
        P("row", ("layer", "col")),
        P(("layer", "row"), "col"),
        P(("layer", "row"), "col"),
    )
    out_specs = P(("row", "layer"), "col")
    return jax.shard_map(
        per_device, mesh=mesh, in_specs=in_specs, out_specs=out_specs, check_vma=False
    )
```

profile of v0, /device:TPU:32, one launch (start us, length us, event | category | flops | bytes accessed | tf_op | source)
XLA Modules:
  0.0 355.3 jit_solution(10024609637868433303)
XLA Ops:
  6.5 0.0 all-gather.3.cloned.1.call-start
  6.5 0.7 convert_element_type.6
  7.2 0.1 copy.5
  7.3 0.3 mul.22
  7.7 2.3 bitcast_multiply_fusion.1
  10.0 0.0 all-gather.3.cloned.1.call-update
  10.0 0.0 all-gather.5.cloned.1.call-start
  10.1 0.7 convert_element_type.7
  10.8 0.2 mul.25
  11.0 2.5 bitcast_multiply_fusion
  13.5 0.0 all-gather.5.cloned.1.call-update
  13.5 0.0 reduce-scatter.2.cloned.1.call-start
  13.6 83.1 %all-gather.3.cloned.1.call-done = bf16[1024,2048]{1,0:T(8,128)(2,1)} async-done(((bf16[1024,512]{1,0:T(8,128)(2,1)}), bf16[1024,2048]{1,0:T(8,128)(2,1)}) %all-gather.3.cloned.1.call-update) | async-done | bytes 4194320 | tf_op jit(solution)/shard_map/all_gather | solution.py:21
  96.7 54.2 %all-gather.5.cloned.1.call-done = bf16[2048,2048]{1,0:T(8,128)(2,1)} async-done(((bf16[256,2048]{1,0:T(8,128)(2,1)}), bf16[2048,2048]{1,0:T(8,128)(2,1)}) %all-gather.5.cloned.1.call-update) | async-done | bytes 8388624 | tf_op jit(solution)/shard_map/all_gather | solution.py:19
  150.9 14.5 %fusion = f32[1024,2048]{1,0:T(8,128)} fusion(bf16[1024,2048]{1,0:T(8,128)(2,1)} %all-gather.3.cloned.1.call-done, bf16[2048,2048]{1,0:T(8,128)(2,1)} %all-gather.5.cloned.1.call-done), kind=kOutput, calls=%fused_computation.2 | convolution fusion | flops 8589934592 | bytes 20971520 | tf_op jit(solution)/shard_map/dot_general | solution.py:20
  165.4 0.0 reduce-scatter.2.cloned.1.call-update
  165.5 183.3 %reduce-scatter.2.cloned.1.call-done = f32[128,2048]{1,0:T(8,128)} async-done(((f32[1024,2048]{1,0:T(8,128)}), f32[128,2048]{1,0:T(8,128)}) %reduce-scatter.2.cloned.1.call-update) | async-done | bytes 1048592 | tf_op jit(solution)/shard_map/reduce_scatter | solution.py:25
Async XLA Ops:
  6.5 90.2 %all-gather.3.cloned.1.call-start = ((), (), s32[]{:S(2)}) async-start(), calls=%async_computation.1 | async-start | bytes 5242880 | tf_op jit(solution)/shard_map/all_gather | solution.py:21
  10.0 140.9 %all-gather.5.cloned.1.call-start = ((), (), s32[]{:S(2)}) async-start(), calls=%async_computation.2 | async-start | bytes 9437184 | tf_op jit(solution)/shard_map/all_gather | solution.py:19
  13.5 335.2 %reduce-scatter.2.cloned.1.call-start = ((), (), s32[]{:S(2)}) async-start(), calls=%async_computation.3 | async-start | bytes 9437184 | tf_op jit(solution)/shard_map/reduce_scatter | solution.py:25
Sparse Core Ops, SparseCore 0:
  10.2 86.4 all-gather.2
  98.6 52.3 all-gather.4
  165.6 183.1 reduce-scatter.1
where the time goes:
time: 355 us
  waiting for transfers between devices  321 us (90%)
  matrix products  14.5 us (4%)
  between operations  13.1 us (4%)
  other arithmetic  6.23 us (2%)
    reduce_scatter x1, waiting for transfers between devices, per_device(): lax.psum_scatter(partial_value, 'layer', scatter_dimension=0, tiled=True)  183 us
    all_gather x1, waiting for transfers between devices, per_device(): lax.all_gather(a_kept, 'col', axis=1, tiled=True)  83.1 us
    all_gather x1, waiting for transfers between devices, per_device(): b_slab = lax.all_gather(b_kept, 'row', axis=0, tiled=True)  54.2 us
    dot_general x1, matrix products, per_device(): jnp.dot(lax.all_gather(a_kept, 'col', axis=1, tiled=True), b_slab, prefer...  14.5 us
  transfers between devices with their start and end apart: 3, of which 3 were waited for; matrix products, arithmetic and copies ran while one was open for 1% of the time, Pallas kernels for 0%

commit v1 on v0

--- a/solution.py
+++ b/solution.py
@@ -16,7 +16,9 @@
 def per_device(a_tiles, a_occupancy, b_tiles, b_occupancy):
     a_kept = keep_blocks(a_tiles, a_occupancy)
     b_kept = keep_blocks(b_tiles, b_occupancy)
-    b_slab = lax.all_gather(b_kept, "row", axis=0, tiled=True)
+    b_slab = jnp.concatenate(
+        lax.all_to_all(jnp.stack([b_kept] * lax.axis_size("row")), "row", 0, 0), axis=0
+    )
     partial_value = jnp.dot(
         lax.all_gather(a_kept, "col", axis=1, tiled=True),
         b_slab,

time: 355 us -> 318 us (0.90)
  waiting for transfers between devices: 321 us -> 276 us
  starting transfers between devices: 0.09 us -> 5.15 us
  local copies, waits for them, and re-layouts: 0.64 us -> 4.93 us
    all_gather x1 -> x0, waiting for transfers between devices: 54.2 us -> none  [per_device(): b_slab = lax.all_gather(b_kept, 'row', axis=0, tiled=True)]
    all_to_all x0 -> x1, starting transfers between devices: none -> 5.07 us  [per_device(): lax.all_to_all(jnp.stack([b_kept] * lax.axis_size('row')), 'row', 0, 0)]
    all_to_all x0 -> x1, waiting for transfers between devices: none -> 5.04 us  [per_device(): lax.all_to_all(jnp.stack([b_kept] * lax.axis_size('row')), 'row', 0, 0)]
    all_gather x1, waiting for transfers between devices: 83.1 us -> 87.8 us  [per_device(): lax.all_gather(a_kept, 'col', axis=1, tiled=True)]
    another operation x0 -> x1, local copies, waits for them, and re-layouts: none -> 4.28 us  [per_device(): jnp.stack([b_kept] * lax.axis_size('row'))]
  transfers between devices with their start and end apart: 3 -> 3, of which waited for: 3 -> 3; matrix products, arithmetic and copies ran while one was open for 1% -> 0% of each run, Pallas kernels for 0% -> 0%
where the time goes in v1:
time: 318 us; the launch traced here: 317 us
  waiting for transfers between devices  276 us (87%)
  matrix products  14.4 us (5%)
  between operations  13.5 us (4%)
  starting transfers between devices  5.15 us (2%)
  local copies, waits for them, and re-layouts  4.93 us (2%)
  other arithmetic  3.28 us (1%)
    reduce_scatter x1, waiting for transfers between devices, per_device(): lax.psum_scatter(partial_value, 'layer', scatter_dimension=0, tiled=True)  183 us
    all_gather x1, waiting for transfers between devices, per_device(): lax.all_gather(a_kept, 'col', axis=1, tiled=True)  87.8 us
    dot_general x1, matrix products, per_device(): jnp.dot(lax.all_gather(a_kept, 'col', axis=1, tiled=True), b_slab, prefer...  14.4 us
  transfers between devices with their start and end apart: 3, of which 3 were waited for; matrix products, arithmetic and copies ran while one was open for 0% of the time, Pallas kernels for 0%

profile of v1, /device:TPU:32, one launch (start us, length us, event | category | flops | bytes accessed | tf_op | source)
XLA Modules:
  0.0 317.3 jit_solution(12663031770164171315)
XLA Ops:
  6.5 0.7 convert_element_type.7
  7.2 0.2 mul.26
  7.4 1.5 bitcast_multiply_fusion
  8.9 4.3 %stack.3 = bf16[8,256,2048]{2,1,0:T(8,128)(2,1)} broadcast(bf16[256,2048]{1,0:T(8,128)(2,1)S(1)} %bitcast_multiply_fusion), dimensions={1,2} | broadcast | bytes 9437184 | tf_op jit(solution)/shard_map/stack | solution.py:20
  13.2 0.0 copy-start.1
  13.2 0.0 copy-start
  13.2 5.1 %all-to-all-start = ((bf16[8,256,2048]{2,1,0:T(8,128)(2,1)}), bf16[8,256,2048]{2,1,0:T(8,128)(2,1)}, u32[]{:S(2)}, u32[]{:S(2)}) async-start(bf16[8,256,2048]{2,1,0:T(8,128)(2,1)} %stack.3), calls=%async_computation | async-start | bytes 16777216 | tf_op jit(solution)/shard_map/all_to_all | solution.py:20
  18.3 0.0 all-gather.2.cloned.1.call-start
  18.3 0.0 copy-done.1
  18.3 0.1 copy.5
  18.4 0.3 mul.23
  18.8 0.0 copy-done
  18.8 1.1 bitcast_multiply_fusion.1
  19.9 0.0 all-gather.2.cloned.1.call-update
  19.9 0.0 reduce-scatter.2.cloned.1.call-start
  20.0 87.8 %all-gather.2.cloned.1.call-done = bf16[1024,2048]{1,0:T(8,128)(2,1)} async-done(((bf16[1024,512]{1,0:T(8,128)(2,1)}), bf16[1024,2048]{1,0:T(8,128)(2,1)}) %all-gather.2.cloned.1.call-update) | async-done | bytes 4194320 | tf_op jit(solution)/shard_map/all_gather | solution.py:23
  107.8 5.0 %all-to-all-done = bf16[8,256,2048]{2,1,0:T(8,128)(2,1)} async-done(((bf16[8,256,2048]{2,1,0:T(8,128)(2,1)}), bf16[8,256,2048]{2,1,0:T(8,128)(2,1)}, u32[]{:S(2)}, u32[]{:S(2)}) %all-to-all-start) | async-done | bytes 8388640 | tf_op jit(solution)/shard_map/all_to_all | solution.py:20
  112.8 14.4 %fusion = f32[1024,2048]{1,0:T(8,128)} fusion(bf16[1024,2048]{1,0:T(8,128)(2,1)} %all-gather.2.cloned.1.call-done, bf16[2048,2048]{1,0:T(8,128)(2,1)} %bitcast), kind=kOutput, calls=%fused_computation.2 | convolution fusion | flops 8589934592 | bytes 20971520 | tf_op jit(solution)/shard_map/dot_general | solution.py:22
  127.3 0.0 reduce-scatter.2.cloned.1.call-update
  127.3 183.2 %reduce-scatter.2.cloned.1.call-done = f32[128,2048]{1,0:T(8,128)} async-done(((f32[1024,2048]{1,0:T(8,128)}), f32[128,2048]{1,0:T(8,128)}) %reduce-scatter.2.cloned.1.call-update) | async-done | bytes 1048592 | tf_op jit(solution)/shard_map/reduce_scatter | solution.py:27
  (1 shorter events, 0.0 us)
Async XLA Ops:
  13.2 5.1 %copy-start.1 = (s32[8,4]{0,1:T(4,128)S(1)}, s32[8,4]{0,1:T(4,128)}, u32[]{:S(2)}) copy-start(s32[8,4]{0,1:T(4,128)} %param.5) | copy-start | bytes 388
  13.2 5.6 %copy-start = (bf16[1024,512]{1,0:T(8,128)(2,1)S(1)}, bf16[1024,512]{1,0:T(8,128)(2,1)}, u32[]{:S(2)}) copy-start(bf16[1024,512]{1,0:T(8,128)(2,1)} %param.4) | copy-start | bytes 3145732
  13.2 99.7 %all-to-all-start = ((bf16[8,256,2048]{2,1,0:T(8,128)(2,1)}), bf16[8,256,2048]{2,1,0:T(8,128)(2,1)}, u32[]{:S(2)}, u32[]{:S(2)}) async-start(bf16[8,256,2048]{2,1,0:T(8,128)(2,1)} %stack.3), calls=%async_computation | async-start | bytes 16777216 | tf_op jit(solution)/shard_map/all_to_all | solution.py:20
  18.3 89.5 %all-gather.2.cloned.1.call-start = ((), (), s32[]{:S(2)}) async-start(), calls=%async_computation.2 | async-start | bytes 5242880 | tf_op jit(solution)/shard_map/all_gather | solution.py:23
  19.9 290.5 %reduce-scatter.2.cloned.1.call-start = ((), (), s32[]{:S(2)}) async-start(), calls=%async_computation.3 | async-start | bytes 9437184 | tf_op jit(solution)/shard_map/reduce_scatter | solution.py:27
Sparse Core Ops, SparseCore 0:
  20.9 86.8 all-gather.1
  127.4 183.0 reduce-scatter.1
